TPU v7x, 32 devices: a whole 2x2x4 slice. The times are simulated.
32 devices in a mesh: seq: 8 (over z, y), head: 4 (over x, core).
Axes of the slice: x: 2, y: 2, z: 4, core: 2. Of those that a mesh axis runs over, the one named last changes fastest.
Arguments:
- queries: bfloat16 [8192, 512], P(('seq', 'head')), may hold values from -6 to 6
- key_rows: bfloat16 [8192, 128], P(('seq', 'head')), may hold values from -6 to 6
- value_rows: bfloat16 [8192, 128], P(('seq', 'head')), may hold values from -6 to 6
- out_grad: bfloat16 [8192, 512], P(('seq', 'head')), may hold values from -6 to 6
- doc_start: int32 [32], replicated, may hold values from 0 to 255
Outputs:
- outputs: bfloat16 [8192, 512], P(('seq', 'head'))
- query_grad: bfloat16 [8192, 512], P(('seq', 'head'))
- key_grad: bfloat16 [8192, 128], P(('seq', 'head'))
- value_grad: bfloat16 [8192, 128], P(('seq', 'head'))
Inputs may be any that keep to these rules, and one draw needn't show every extreme that they name: doc_start[c] is the position within span c of the first token of a new document.
All inputs are finite; a program needn't handle non-finite values.
Results may differ from a plain program's by a relative error of at most 0.0065.
Values may be sent and summed in bfloat16 or wider, within the bound.
No kernel may reach another device: no remote copies, remote signals or barrier semaphores. Data moves between devices by JAX's collectives and lax.ppermute only.
A program may use at most 128 MiB of HBM per device.

v0:
```python
import math
import jax
import jax.numpy as jnp
from jax import lax
from jax.sharding import PartitionSpec as P

HD = 128
GROUP = 4
SPANS_DEV = 4
masked_fill = -1e30


def passed_along(value, axis, steps):
    count = lax.axis_size(axis)
    first, last = (max(0, -steps), min(count, count - steps))
    return lax.ppermute(value, axis, [(source, source + steps) for source in range(first, last)])


def allowed_mask(
    first_row, row_count, key_count, halo_len, span_len, span_start, prev_begin, span_index
):
    row_pos = first_row + lax.broadcasted_iota(jnp.int32, (row_count, key_count), 0)
    col_pos = lax.broadcasted_iota(jnp.int32, (row_count, key_count), 1) - halo_len
    return (
        (col_pos <= row_pos)
        & ((col_pos >= span_start) | (span_start > row_pos))
        & (col_pos >= prev_begin - span_len)
        & ((col_pos >= 0) | (span_index > 0))
    )


def attend(query_rows, grad_rows, key_block, value_block, allowed, head_dim):
    score_scale = 1.0 / math.sqrt(head_dim)
    contract = (((2,), (2,)), ((0,), (0,)))
    forward = (((2,), (1,)), ((0,), (0,)))
    backward = (((1,), (1,)), ((0,), (0,)))
    scores = (
        lax.dot_general(query_rows, key_block, contract, preferred_element_type=jnp.float32)
        * score_scale
    )
    masked = jnp.where(allowed, scores, masked_fill)
    row_max = jnp.max(masked, axis=2, keepdims=True)
    exp_scores = jnp.where(allowed, jnp.exp(masked - row_max), 0.0)
    weights = exp_scores / jnp.sum(exp_scores, axis=2, keepdims=True)
    weights_low = weights.astype(jnp.bfloat16)
    result = lax.dot_general(
        weights_low, value_block, forward, preferred_element_type=jnp.float32
    ).astype(jnp.bfloat16)
    grad_weights = lax.dot_general(
        grad_rows, value_block, contract, preferred_element_type=jnp.float32
    )
    row_delta = jnp.sum(weights * grad_weights, axis=2, keepdims=True)
    grad_scores = (weights * (grad_weights - row_delta) * score_scale).astype(jnp.bfloat16)
    grad_query = lax.dot_general(
        grad_scores, key_block, forward, preferred_element_type=jnp.float32
    )
    grad_key = lax.dot_general(
        grad_scores, query_rows, backward, preferred_element_type=jnp.float32
    )
    grad_value = lax.dot_general(
        weights_low, grad_rows, backward, preferred_element_type=jnp.float32
    )
    return (result, grad_query, grad_key, grad_value)


def per_device(queries, key_rows, value_rows, out_grad, doc_start):
    tok_count = queries.shape[0]
    head_count = lax.axis_size("head")
    group_rows = tok_count * head_count
    span_len = group_rows // SPANS_DEV
    halo_len = span_len // 4
    half_len = span_len // 2
    rest_len = span_len - halo_len
    head_q, head_grad = (
        lax.all_to_all(queries, "head", split_axis=1, concat_axis=0, tiled=True),
        lax.all_to_all(out_grad, "head", split_axis=1, concat_axis=0, tiled=True),
    )
    full_k, full_v = (
        lax.all_gather(key_rows, "head", axis=0, tiled=True),
        lax.all_gather(value_rows, "head", axis=0, tiled=True),
    )
    column = lax.axis_index("head") // GROUP * HD
    head_k = lax.dynamic_slice_in_dim(full_k, column, HD, 1)
    head_v = lax.dynamic_slice_in_dim(full_v, column, HD, 1)
    query_3 = head_q.reshape(SPANS_DEV, span_len, HD)
    grad_3 = head_grad.reshape(SPANS_DEV, span_len, HD)
    keys_3 = head_k.reshape(SPANS_DEV, span_len, HD)
    values_3 = head_v.reshape(SPANS_DEV, span_len, HD)
    tail_k = keys_3[:, rest_len:]
    tail_v = values_3[:, rest_len:]
    edge_last_k, edge_last_v = passed_along(
        (tail_k[SPANS_DEV - 1], tail_v[SPANS_DEV - 1]), "seq", 1
    )
    edge_k = jnp.concatenate([edge_last_k[None], tail_k[: SPANS_DEV - 1]], axis=0)
    edge_v = jnp.concatenate([edge_last_v[None], tail_v[: SPANS_DEV - 1]], axis=0)
    key_block = jnp.concatenate([edge_k, keys_3], axis=1)
    value_block = jnp.concatenate([edge_v, values_3], axis=1)
    first_span = lax.axis_index("seq") * SPANS_DEV
    span_starts = lax.dynamic_slice_in_dim(doc_start, first_span, SPANS_DEV)
    before_start = lax.dynamic_slice_in_dim(doc_start, jnp.maximum(first_span - 1, 0), 1)
    prev_starts = jnp.concatenate([before_start, span_starts[: SPANS_DEV - 1]], axis=0)
    span_ids = first_span + jnp.arange(SPANS_DEV, dtype=jnp.int32)
    span_starts = span_starts.reshape(SPANS_DEV, 1, 1)
    prev_starts = prev_starts.reshape(SPANS_DEV, 1, 1)
    span_ids = span_ids.reshape(SPANS_DEV, 1, 1)
    grad_key = jnp.zeros((SPANS_DEV, halo_len + span_len, HD), jnp.float32)
    grad_value = jnp.zeros((SPANS_DEV, halo_len + span_len, HD), jnp.float32)
    results = []
    query_grads = []
    for block_index in range(2):
        first_row = block_index * half_len
        key_count = halo_len + first_row + half_len
        allowed = allowed_mask(
            first_row, half_len, key_count, halo_len, span_len, span_starts, prev_starts, span_ids
        )
        result, grad_query, part_key, part_value = attend(
            query_3[:, first_row : first_row + half_len],
            grad_3[:, first_row : first_row + half_len],
            key_block[:, :key_count],
            value_block[:, :key_count],
            allowed,
            HD,
        )
        results.append(result)
        query_grads.append(grad_query.astype(jnp.bfloat16))
        grad_key = grad_key.at[:, :key_count].add(part_key)
        grad_value = grad_value.at[:, :key_count].add(part_value)
    next_last_k, next_last_v = passed_along(
        (grad_key[0, :halo_len], grad_value[0, :halo_len]), "seq", -1
    )
    next_k = jnp.concatenate([grad_key[1:, :halo_len], next_last_k[None]], axis=0)
    next_v = jnp.concatenate([grad_value[1:, :halo_len], next_last_v[None]], axis=0)
    own_k = jnp.concatenate(
        [grad_key[:, halo_len : halo_len + rest_len], grad_key[:, halo_len + rest_len :] + next_k],
        axis=1,
    ).reshape(group_rows, HD)
    own_v = jnp.concatenate(
        [
            grad_value[:, halo_len : halo_len + rest_len],
            grad_value[:, halo_len + rest_len :] + next_v,
        ],
        axis=1,
    ).reshape(group_rows, HD)
    all_results = jnp.concatenate(results, axis=1).reshape(group_rows, HD)
    all_query_grads = jnp.concatenate(query_grads, axis=1).reshape(group_rows, HD)
    outputs, query_grad = (
        lax.all_to_all(all_results, "head", split_axis=0, concat_axis=1, tiled=True),
        lax.all_to_all(all_query_grads, "head", split_axis=0, concat_axis=1, tiled=True),
    )
    wide_gk, wide_gv = (
        lax.all_to_all(own_k, "head", split_axis=0, concat_axis=1, tiled=True),
        lax.all_to_all(own_v, "head", split_axis=0, concat_axis=1, tiled=True),
    )
    group_total = wide_gk.shape[1] // (GROUP * HD)
    key_grad = (
        wide_gk.reshape(tok_count, group_total, GROUP, HD)
        .sum(axis=2)
        .reshape(tok_count, group_total * HD)
        .astype(jnp.bfloat16)
    )
    value_grad = (
        wide_gv.reshape(tok_count, group_total, GROUP, HD)
        .sum(axis=2)
        .reshape(tok_count, group_total * HD)
        .astype(jnp.bfloat16)
    )
    return (outputs, query_grad, key_grad, value_grad)


def solution(mesh):
    placed = (
        P(("seq", "head"), None),
        P(("seq", "head"), None),
        P(("seq", "head"), None),
        P(("seq", "head"), None),
        P(),
    )
    return jax.shard_map(
        per_device,
        mesh=mesh,
        in_specs=placed,
        out_specs=(
            P(("seq", "head"), None),
            P(("seq", "head"), None),
            P(("seq", "head"), None),
            P(("seq", "head"), None),
        ),
        check_vma=False,
    )
```

profile of v0, /device:TPU:8, one launch (start us, length us, event | category | flops | bytes accessed | tf_op | source)
XLA Modules:
  0.0 94.2 jit_solution(2533710951645964501)
XLA Ops:
  0.6 0.0 copy-start.2
  0.6 6.1 %all_gather.7 = bf16[1024,128]{1,0:T(8,128)(2,1)S(1)} all-gather(bf16[256,128]{1,0:T(8,128)(2,1)} %param.19), channel_id=1, replica_groups=mesh['seq'=8,'head'=4] {'head'}, dimensions={0}, use_global_device_ids=true | all-gather | bytes 327680 | tf_op jit(solution)/shard_map/all_gather | solution.py:80
  6.8 3.5 %collective-permute-start.1 = (bf16[64,128]{1,0:T(8,128)(2,1)S(1)}, bf16[64,128]{1,0:T(8,128)(2,1)S(1)}, u32[]{:S(2)}, u32[]{:S(2)}) collective-permute-start(bf16[64,128]{1,0:T(8,128)(2,1)S(1)} %slice_bitcast_fusion.2), channel_id=1, source_target_pairs={{0,4},{4,8},{8,12},{12,16},{16,20},{20,24},{24,28},{1,5},{5,9},{9,... | collective-permute-start | bytes 49160 | tf_op jit(solution)/shard_map/ppermute | solution.py:16
  10.3 0.0 copy-done.2
  10.3 5.8 %all_gather.6 = bf16[1024,128]{1,0:T(8,128)(2,1)S(1)} all-gather(bf16[256,128]{1,0:T(8,128)(2,1)S(1)} %copy-done.2), channel_id=1, replica_groups=mesh['seq'=8,'head'=4] {'head'}, dimensions={0}, use_global_device_ids=true | all-gather | bytes 327680 | tf_op jit(solution)/shard_map/all_gather | solution.py:79
  16.1 3.4 %collective-permute-start = (bf16[64,128]{1,0:T(8,128)(2,1)S(1)}, bf16[64,128]{1,0:T(8,128)(2,1)S(1)}, u32[]{:S(2)}, u32[]{:S(2)}) collective-permute-start(bf16[64,128]{1,0:T(8,128)(2,1)S(1)} %slice_bitcast_fusion.3), channel_id=1, source_target_pairs={{0,4},{4,8},{8,12},{12,16},{16,20},{20,24},{24,28},{1,5},{5,9},{9,... | collective-permute-start | bytes 49160 | tf_op jit(solution)/shard_map/ppermute | solution.py:16
  19.6 0.0 copy-done
  19.6 0.1 copy.12
  19.7 0.8 copy.13
  20.6 3.5 %all-to-all-start.2 = ((bf16[256,4,128]{2,0,1:T(8,128)(2,1)}), bf16[256,4,128]{2,0,1:T(8,128)(2,1)S(1)}, u32[]{:S(2)}, u32[]{:S(2)}) async-start(bf16[256,4,128]{2,0,1:T(8,128)(2,1)} %copy.13), calls=%async_computation.2 | async-start | bytes 524288 | tf_op jit(solution)/shard_map/all_to_all | solution.py:76
  24.1 0.0 copy-start.1
  24.1 0.0 copy-start.11
  24.2 0.0 copy-start.9
  24.2 0.1 dynamic_slice.8
  24.3 0.6 dynamic_slice.9
  24.9 0.1 iota_compare_fusion.1
  25.0 0.1 broadcast_compare_fusion
  25.1 0.0 copy-start.5
  25.1 0.7 add_add_fusion
  25.9 0.0 copy-start.3
  25.9 0.1 copy.9
  26.0 0.8 copy.10
  26.9 3.2 %all-to-all-done.2 = bf16[256,4,128]{2,0,1:T(8,128)(2,1)S(1)} async-done(((bf16[256,4,128]{2,0,1:T(8,128)(2,1)}), bf16[256,4,128]{2,0,1:T(8,128)(2,1)S(1)}, u32[]{:S(2)}, u32[]{:S(2)}) %all-to-all-start.2) | async-done | bytes 262176 | tf_op jit(solution)/shard_map/all_to_all | solution.py:76
  30.1 3.4 %all-to-all-start = ((bf16[256,4,128]{2,0,1:T(8,128)(2,1)}), bf16[256,4,128]{2,0,1:T(8,128)(2,1)S(1)}, u32[]{:S(2)}, u32[]{:S(2)}) async-start(bf16[256,4,128]{2,0,1:T(8,128)(2,1)} %copy.10), calls=%async_computation | async-start | bytes 524288 | tf_op jit(solution)/shard_map/all_to_all | solution.py:75
  33.5 0.0 collective-permute-done.1
  33.5 0.2 convolution_bitcast_fusion
  33.8 0.2 convolution_bitcast_fusion.1
  34.0 0.0 collective-permute-done
  34.0 0.0 copy-start.6
  34.0 5.5 %all-to-all-done = bf16[256,4,128]{2,0,1:T(8,128)(2,1)S(1)} async-done(((bf16[256,4,128]{2,0,1:T(8,128)(2,1)}), bf16[256,4,128]{2,0,1:T(8,128)(2,1)S(1)}, u32[]{:S(2)}, u32[]{:S(2)}) %all-to-all-start) | async-done | bytes 262176 | tf_op jit(solution)/shard_map/all_to_all | solution.py:75
  39.5 0.5 fusion.106
  40.0 0.7 convolution_convert_fusion.3
  40.7 1.3 %fusion.43 = f32[4,192,128]{2,1,0:T(8,128)} fusion(bf16[4,256,128]{2,1,0:T(8,128)(2,1)S(1)} %bitcast.71, f32[4,128]{1,0:T(4,128)S(1)} %get-tuple-element.74, bf16[4,256,128]{2,1,0:T(8,128)(2,1)S(1)} %bitcast.91, bf16[4,256,128]{2,1,0:T(8,128)(2,1)S(1)} %bitcast.83, bf16[3,64,128]{2,1,0:T(8,128)(2,1)S(1)} %slice.163, bf16[1,64,128]{2,1,0:T(8,128)(2,1)S(1)} %bitcast.105, ...), kind=kOutput, calls=%fused_computation.65 | convolution fusion | flops 53084864 | bytes 1040384 | tf_op jit(solution)/shard_map/dot_general | solution.py:60
  42.0 1.5 %fusion.103 = (f32[4,128]{1,0:T(4,128)S(1)}, f32[4,128,320]{1,2,0:T(8,128)}) fusion(bf16[4,256,128]{2,1,0:T(8,128)(2,1)S(1)} %bitcast.84, bf16[3,64,128]{2,1,0:T(8,128)(2,1)S(1)} %slice.163, bf16[1,64,128]{2,1,0:T(8,128)(2,1)S(1)} %bitcast.106, bf16[4,256,128]{2,1,0:T(8,128)(2,1)S(1)} %bitcast.92, pred[4]{0:T(512)(128)(4,1)S(1)} %add_compare_fusion, ...), kind=kOutput, calls=%fused_computation.111 | convolution fusion | flops 46367040 | bytes 1207296 | tf_op jit(solution)/shard_map/sub | solution.py:43
  43.6 0.0 copy-done.5
  43.6 0.9 %convolution_convert_fusion.2 = bf16[4,128,128]{2,1,0:T(8,128)(2,1)S(1)} fusion(bf16[4,256,128]{2,1,0:T(8,128)(2,1)S(1)} %bitcast.68, bf16[3,64,128]{2,1,0:T(8,128)(2,1)S(1)} %slice.166, bf16[1,64,128]{2,1,0:T(8,128)(2,1)S(1)} %bitcast.100, f32[4,128]{1,0:T(4,128)S(1)} %get-tuple-element.72, bf16[4,256,128]{2,1,0:T(8,128)(2,1)S(1)} %bitcast.85, ...), kind=kOutput, calls=%fused_computation.30 | convolution fusion | flops 89523008 | bytes 1010688 | tf_op jit(solution)/shard_map/dot_general | solution.py:46
  44.5 0.7 pad_maximum_fusion.4
  45.3 3.4 %all-to-all-start.1 = ((bf16[4,256,128]{2,1,0:T(8,128)(2,1)}), bf16[4,256,128]{2,1,0:T(8,128)(2,1)S(1)}, u32[]{:S(2)}, u32[]{:S(2)}) async-start(bf16[4,256,128]{2,1,0:T(8,128)(2,1)} %pad_maximum_fusion.4), calls=%async_computation.1 | async-start | bytes 524288 | tf_op jit(solution)/shard_map/all_to_all | solution.py:147
  48.7 1.7 %convolution_convert_fusion = bf16[4,128,128]{2,1,0:T(8,128)(2,1)S(1)} fusion(f32[4,128,320]{1,2,0:T(8,128)S(1)} %convolution_bitcast_fusion, bf16[4,256,128]{2,1,0:T(8,128)(2,1)S(1)} %bitcast.86, bf16[3,64,128]{2,1,0:T(8,128)(2,1)S(1)} %slice.163, bf16[1,64,128]{2,1,0:T(8,128)(2,1)S(1)} %bitcast.108, f32[4,128,320]{1,2,0:T(8,128)} %get-tuple-element.73, ...), kind=kOutput, calls=%fused_computation.28 | convolution fusion | flops 44139328 | bytes 1771520 | tf_op jit(solution)/shard_map/dot_general | solution.py:54
  50.4 1.0 %fusion.22 = f32[4,192,128]{2,1,0:T(8,128)} fusion(f32[4,128,192]{1,2,0:T(8,128)S(1)} %convolution_bitcast_fusion.1, bf16[4,256,128]{2,1,0:T(8,128)(2,1)S(1)} %bitcast.94, f32[4,128,192]{1,2,0:T(8,128)S(1)} %get-tuple-element.75, f32[4,128]{1,0:T(4,128)S(1)} %get-tuple-element.74), kind=kOutput, calls=%fused_computation.32 | convolution fusion | flops 25854656 | bytes 2101248 | tf_op jit(solution)/shard_map/dot_general | solution.py:57
  51.4 1.7 %convolution_add_fusion.1 = f32[4,320,128]{2,1,0:T(8,128)S(1)} fusion(f32[4,128,320]{1,2,0:T(8,128)S(1)} %convolution_bitcast_fusion, f32[4,192,128]{2,1,0:T(8,128)} %fusion.22, bf16[4,256,128]{2,1,0:T(8,128)(2,1)S(1)} %bitcast.95, f32[4,128,320]{1,2,0:T(8,128)} %get-tuple-element.73, f32[4,128]{1,0:T(4,128)S(1)} %get-tuple-element.72), kind=kOutput, calls=%fused_computation.11 | convolution fusion | flops 43254592 | bytes 3805184 | tf_op jit(solution)/shard_map/dot_general | solution.py:57
  53.2 0.0 copy-start.7
  53.2 3.3 %collective-permute-start.2 = (f32[64,128]{1,0:T(8,128)S(1)}, f32[64,128]{1,0:T(8,128)S(1)}, u32[]{:S(2)}, u32[]{:S(2)}) collective-permute-start(f32[64,128]{1,0:T(8,128)S(1)} %slice_bitcast_fusion.1), channel_id=1, source_target_pairs={{4,0},{8,4},{12,8},{16,12},{20,16},{24,20},{28,24},{5,1},{9,5},{13... | collective-permute-start | bytes 98312 | tf_op jit(solution)/shard_map/ppermute | solution.py:16
  56.6 1.9 %convolution_add_fusion = f32[4,320,128]{2,1,0:T(8,128)S(1)} fusion(f32[4,192,128]{2,1,0:T(8,128)} %fusion.43, bf16[4,256,128]{2,1,0:T(8,128)(2,1)S(1)} %bitcast.72, f32[4,128]{1,0:T(4,128)S(1)} %get-tuple-element.72, bf16[4,256,128]{2,1,0:T(8,128)(2,1)S(1)} %bitcast.87, bf16[3,64,128]{2,1,0:T(8,128)(2,1)S(1)} %copy-done.4, ...), kind=kOutput, calls=%fused_computation.10 | convolution fusion | flops 88638272 | bytes 1731584 | tf_op jit(solution)/shard_map/dot_general | solution.py:60
  58.4 0.4 convolution_convert_fusion.1
  58.8 0.7 pad_maximum_fusion.5
  59.6 0.0 all-to-all-done.1
  59.6 3.4 %all-to-all-start.3 = ((bf16[4,256,128]{2,1,0:T(8,128)(2,1)}), bf16[4,256,128]{2,1,0:T(8,128)(2,1)S(1)}, u32[]{:S(2)}, u32[]{:S(2)}) async-start(bf16[4,256,128]{2,1,0:T(8,128)(2,1)} %pad_maximum_fusion.5), calls=%async_computation.3 | async-start | bytes 524288 | tf_op jit(solution)/shard_map/all_to_all | solution.py:148
  63.0 0.0 collective-permute-done.2
  63.0 0.8 pad_maximum_fusion
  63.9 5.1 %all-to-all-done.3 = bf16[4,256,128]{2,1,0:T(8,128)(2,1)S(1)} async-done(((bf16[4,256,128]{2,1,0:T(8,128)(2,1)}), bf16[4,256,128]{2,1,0:T(8,128)(2,1)S(1)}, u32[]{:S(2)}, u32[]{:S(2)}) %all-to-all-start.3) | async-done | bytes 262176 | tf_op jit(solution)/shard_map/all_to_all | solution.py:148
  69.0 3.5 %all-to-all-start.4 = ((f32[4,256,128]{2,1,0:T(8,128)}), f32[4,256,128]{2,1,0:T(8,128)S(1)}, u32[]{:S(2)}, u32[]{:S(2)}) async-start(f32[4,256,128]{2,1,0:T(8,128)} %pad_maximum_fusion), calls=%async_computation.4 | async-start | bytes 1048576 | tf_op jit(solution)/shard_map/all_to_all | solution.py:151
  72.5 2.4 %collective-permute-start.3 = (f32[64,128]{1,0:T(8,128)S(1)}, f32[64,128]{1,0:T(8,128)S(1)}, u32[]{:S(2)}, u32[]{:S(2)}) collective-permute-start(f32[64,128]{1,0:T(8,128)S(1)} %slice_bitcast_fusion), channel_id=1, source_target_pairs={{4,0},{8,4},{12,8},{16,12},{20,16},{24,20},{28,24},{5,1},{9,5},{13... | collective-permute-start | bytes 98312 | tf_op jit(solution)/shard_map/ppermute | solution.py:16
  75.0 3.3 %collective-permute-done.3 = f32[64,128]{1,0:T(8,128)S(1)} collective-permute-done((f32[64,128]{1,0:T(8,128)S(1)}, f32[64,128]{1,0:T(8,128)S(1)}, u32[]{:S(2)}, u32[]{:S(2)}) %collective-permute-start.3) | collective-permute-done | bytes 32800 | tf_op jit(solution)/shard_map/ppermute | solution.py:16
  78.3 0.8 pad_maximum_fusion.1
  79.2 2.1 %all-to-all-done.4 = f32[4,256,128]{2,1,0:T(8,128)S(1)} async-done(((f32[4,256,128]{2,1,0:T(8,128)}), f32[4,256,128]{2,1,0:T(8,128)S(1)}, u32[]{:S(2)}, u32[]{:S(2)}) %all-to-all-start.4) | async-done | bytes 524320 | tf_op jit(solution)/shard_map/all_to_all | solution.py:151
  81.3 3.5 %all-to-all-start.5 = ((f32[4,256,128]{2,1,0:T(8,128)}), f32[4,256,128]{2,1,0:T(8,128)S(1)}, u32[]{:S(2)}, u32[]{:S(2)}) async-start(f32[4,256,128]{2,1,0:T(8,128)} %pad_maximum_fusion.1), calls=%async_computation.5 | async-start | bytes 1048576 | tf_op jit(solution)/shard_map/all_to_all | solution.py:152
  84.8 0.1 copy.11
  84.9 0.8 copy.15
  85.8 0.1 copy.14
  85.9 0.8 copy.16
  86.8 0.7 reduce_sum.58
  87.4 6.2 %all-to-all-done.5 = f32[4,256,128]{2,1,0:T(8,128)S(1)} async-done(((f32[4,256,128]{2,1,0:T(8,128)}), f32[4,256,128]{2,1,0:T(8,128)S(1)}, u32[]{:S(2)}, u32[]{:S(2)}) %all-to-all-start.5) | async-done | bytes 524320 | tf_op jit(solution)/shard_map/all_to_all | solution.py:152
  93.6 0.7 reduce_sum.59
  (33 shorter events, 0.2 us)
Async XLA Ops:
  0.6 9.7 %copy-start.2 = (bf16[256,128]{1,0:T(8,128)(2,1)S(1)}, bf16[256,128]{1,0:T(8,128)(2,1)}, u32[]{:S(2)}) copy-start(bf16[256,128]{1,0:T(8,128)(2,1)} %param.18) | copy-start | bytes 196612
  6.8 12.8 %copy-start = (bf16[256,512]{1,0:T(8,128)(2,1)S(1)}, bf16[256,512]{1,0:T(8,128)(2,1)}, u32[]{:S(2)}) copy-start(bf16[256,512]{1,0:T(8,128)(2,1)} %param.20) | copy-start | bytes 786436
  6.8 26.7 %collective-permute-start.1 = (bf16[64,128]{1,0:T(8,128)(2,1)S(1)}, bf16[64,128]{1,0:T(8,128)(2,1)S(1)}, u32[]{:S(2)}, u32[]{:S(2)}) collective-permute-start(bf16[64,128]{1,0:T(8,128)(2,1)S(1)} %slice_bitcast_fusion.2), channel_id=1, source_target_pairs={{0,4},{4,8},{8,12},{12,16},{16,20},{20,24},{24,28},{1,5},{5,9},{9,... | collective-permute-start | bytes 49160 | tf_op jit(solution)/shard_map/ppermute | solution.py:16
  16.1 17.9 %collective-permute-start = (bf16[64,128]{1,0:T(8,128)(2,1)S(1)}, bf16[64,128]{1,0:T(8,128)(2,1)S(1)}, u32[]{:S(2)}, u32[]{:S(2)}) collective-permute-start(bf16[64,128]{1,0:T(8,128)(2,1)S(1)} %slice_bitcast_fusion.3), channel_id=1, source_target_pairs={{0,4},{4,8},{8,12},{12,16},{16,20},{20,24},{24,28},{1,5},{5,9},{9,... | collective-permute-start | bytes 49160 | tf_op jit(solution)/shard_map/ppermute | solution.py:16
  20.5 3.7 %copy-start.8 = (s32[32]{0:T(128)S(1)}, s32[32]{0:T(128)}, u32[]{:S(2)}) copy-start(s32[32]{0:T(128)} %param.21) | copy-start | bytes 388
  20.6 9.5 %all-to-all-start.2 = ((bf16[256,4,128]{2,0,1:T(8,128)(2,1)}), bf16[256,4,128]{2,0,1:T(8,128)(2,1)S(1)}, u32[]{:S(2)}, u32[]{:S(2)}) async-start(bf16[256,4,128]{2,0,1:T(8,128)(2,1)} %copy.13), calls=%async_computation.2 | async-start | bytes 524288 | tf_op jit(solution)/shard_map/all_to_all | solution.py:76
  24.1 1.8 %copy-start.1 = (bf16[256,512]{1,0:T(8,128)(2,1)S(1)}, bf16[256,512]{1,0:T(8,128)(2,1)}, u32[]{:S(2)}) copy-start(bf16[256,512]{1,0:T(8,128)(2,1)} %param.17) | copy-start | bytes 786436
  24.1 19.4 %copy-start.11 = (pred[320]{0:T(512)(128)(4,1)}, pred[320]{0:T(512)(128)(4,1)S(1)}, u32[]{:S(2)}) copy-start(pred[320]{0:T(512)(128)(4,1)S(1)} %broadcast_compare_fusion.1) | copy-start | bytes 964
  24.2 19.4 %copy-start.9 = (pred[4]{0:T(512)(128)(4,1)}, pred[4]{0:T(512)(128)(4,1)S(1)}, u32[]{:S(2)}) copy-start(pred[4]{0:T(512)(128)(4,1)S(1)} %add_compare_fusion) | copy-start | bytes 16
  25.1 18.5 %copy-start.5 = (pred[128,320]{0,1:T(8,128)(4,1)}, pred[128,320]{0,1:T(8,128)(4,1)S(1)}, u32[]{:S(2)}) copy-start(pred[128,320]{0,1:T(8,128)(4,1)S(1)} %broadcast_compare_fusion) | copy-start | bytes 122884
  25.9 22.8 %copy-start.3 = (bf16[3,64,128]{2,1,0:T(8,128)(2,1)}, bf16[3,64,128]{2,1,0:T(8,128)(2,1)S(1)}, u32[]{:S(2)}) copy-start(bf16[3,64,128]{2,1,0:T(8,128)(2,1)S(1)} %slice.163) | copy-start | bytes 147460
  30.1 9.4 %all-to-all-start = ((bf16[256,4,128]{2,0,1:T(8,128)(2,1)}), bf16[256,4,128]{2,0,1:T(8,128)(2,1)S(1)}, u32[]{:S(2)}, u32[]{:S(2)}) async-start(bf16[256,4,128]{2,0,1:T(8,128)(2,1)} %copy.10), calls=%async_computation | async-start | bytes 524288 | tf_op jit(solution)/shard_map/all_to_all | solution.py:75
  34.0 14.7 %copy-start.6 = (bf16[64,128]{1,0:T(8,128)(2,1)}, bf16[64,128]{1,0:T(8,128)(2,1)S(1)}, u32[]{:S(2)}) copy-start(bf16[64,128]{1,0:T(8,128)(2,1)S(1)} %collective-permute-done) | copy-start | bytes 49156
  45.3 14.3 %all-to-all-start.1 = ((bf16[4,256,128]{2,1,0:T(8,128)(2,1)}), bf16[4,256,128]{2,1,0:T(8,128)(2,1)S(1)}, u32[]{:S(2)}, u32[]{:S(2)}) async-start(bf16[4,256,128]{2,1,0:T(8,128)(2,1)} %pad_maximum_fusion.4), calls=%async_computation.1 | async-start | bytes 524288 | tf_op jit(solution)/shard_map/all_to_all | solution.py:147
  51.4 5.1 %copy-start.10 = (pred[4]{0:T(512)(128)(4,1)S(1)}, pred[4]{0:T(512)(128)(4,1)}, u32[]{:S(2)}) copy-start(pred[4]{0:T(512)(128)(4,1)} %copy-done.9) | copy-start | bytes 16
  51.4 5.1 %copy-start.12 = (pred[320]{0:T(512)(128)(4,1)S(1)}, pred[320]{0:T(512)(128)(4,1)}, u32[]{:S(2)}) copy-start(pred[320]{0:T(512)(128)(4,1)} %copy-done.11) | copy-start | bytes 964
  53.2 3.4 %copy-start.4 = (bf16[3,64,128]{2,1,0:T(8,128)(2,1)S(1)}, bf16[3,64,128]{2,1,0:T(8,128)(2,1)}, u32[]{:S(2)}) copy-start(bf16[3,64,128]{2,1,0:T(8,128)(2,1)} %copy-done.3) | copy-start | bytes 147460
  53.2 3.4 %copy-start.7 = (bf16[64,128]{1,0:T(8,128)(2,1)S(1)}, bf16[64,128]{1,0:T(8,128)(2,1)}, u32[]{:S(2)}) copy-start(bf16[64,128]{1,0:T(8,128)(2,1)} %copy-done.6) | copy-start | bytes 49156
  53.2 9.8 %collective-permute-start.2 = (f32[64,128]{1,0:T(8,128)S(1)}, f32[64,128]{1,0:T(8,128)S(1)}, u32[]{:S(2)}, u32[]{:S(2)}) collective-permute-start(f32[64,128]{1,0:T(8,128)S(1)} %slice_bitcast_fusion.1), channel_id=1, source_target_pairs={{4,0},{8,4},{12,8},{16,12},{20,16},{24,20},{28,24},{5,1},{9,5},{13... | collective-permute-start | bytes 98312 | tf_op jit(solution)/shard_map/ppermute | solution.py:16
  59.6 9.4 %all-to-all-start.3 = ((bf16[4,256,128]{2,1,0:T(8,128)(2,1)}), bf16[4,256,128]{2,1,0:T(8,128)(2,1)S(1)}, u32[]{:S(2)}, u32[]{:S(2)}) async-start(bf16[4,256,128]{2,1,0:T(8,128)(2,1)} %pad_maximum_fusion.5), calls=%async_computation.3 | async-start | bytes 524288 | tf_op jit(solution)/shard_map/all_to_all | solution.py:148
  69.0 12.3 %all-to-all-start.4 = ((f32[4,256,128]{2,1,0:T(8,128)}), f32[4,256,128]{2,1,0:T(8,128)S(1)}, u32[]{:S(2)}, u32[]{:S(2)}) async-start(f32[4,256,128]{2,1,0:T(8,128)} %pad_maximum_fusion), calls=%async_computation.4 | async-start | bytes 1048576 | tf_op jit(solution)/shard_map/all_to_all | solution.py:151
  72.5 5.8 %collective-permute-start.3 = (f32[64,128]{1,0:T(8,128)S(1)}, f32[64,128]{1,0:T(8,128)S(1)}, u32[]{:S(2)}, u32[]{:S(2)}) collective-permute-start(f32[64,128]{1,0:T(8,128)S(1)} %slice_bitcast_fusion), channel_id=1, source_target_pairs={{4,0},{8,4},{12,8},{16,12},{20,16},{24,20},{28,24},{5,1},{9,5},{13... | collective-permute-start | bytes 98312 | tf_op jit(solution)/shard_map/ppermute | solution.py:16
  81.3 12.3 %all-to-all-start.5 = ((f32[4,256,128]{2,1,0:T(8,128)}), f32[4,256,128]{2,1,0:T(8,128)S(1)}, u32[]{:S(2)}, u32[]{:S(2)}) async-start(f32[4,256,128]{2,1,0:T(8,128)} %pad_maximum_fusion.1), calls=%async_computation.5 | async-start | bytes 1048576 | tf_op jit(solution)/shard_map/all_to_all | solution.py:152
where the time goes:
time: 95.1 us; the launch traced here: 94.2 us
  starting transfers between devices  33.4 us (35%)
  waiting for transfers between devices  25.5 us (27%)
  matrix products  12.1 us (13%)
  blocking collectives  11.9 us (13%)
  other arithmetic  5.42 us (6%)
  local copies, waits for them, and re-layouts  4.74 us (5%)
  between operations  1.09 us (1%)
    ppermute x4, starting transfers between devices, passed_along(): lax.ppermute(value, axis, [(source, source + steps) for source in range(f...  12.7 us
    all_to_all x1, waiting for transfers between devices, per_device(): lax.all_to_all(own_v, 'head', split_axis=0, concat_axis=1, tiled=True)  6.16 us
    all_gather x1, blocking collectives, per_device(): lax.all_gather(value_rows, 'head', axis=0, tiled=True)  6.13 us
    all_gather x1, blocking collectives, per_device(): lax.all_gather(key_rows, 'head', axis=0, tiled=True)  5.79 us
    all_to_all x1, waiting for transfers between devices, per_device(): lax.all_to_all(queries, 'head', split_axis=1, concat_axis=0, tiled=True)  5.5 us
    all_to_all x1, waiting for transfers between devices, per_device(): lax.all_to_all(all_query_grads, 'head', split_axis=0, concat_axis=1, tile...  5.14 us
    all_to_all x1, starting transfers between devices, per_device(): lax.all_to_all(out_grad, 'head', split_axis=1, concat_axis=0, tiled=True)  3.54 us
    all_to_all x1, starting transfers between devices, per_device(): lax.all_to_all(own_v, 'head', split_axis=0, concat_axis=1, tiled=True)  3.47 us
  transfers between devices with their start and end apart: 10, of which 6 were waited for; matrix products, arithmetic and copies ran while one was open for 17% of the time, Pallas kernels for 0%

commit v1 on v0

--- a/solution.py
+++ b/solution.py
@@ -8,6 +8,22 @@
 GROUP = 4
 SPANS_DEV = 4
 masked_fill = -1e30
+
+
+def swapped_with_each(array, axis, split, join):
+    ways, here = (lax.axis_size(axis), lax.axis_index(axis))
+    width = array.shape[split] // ways
+    lengths = list(array.shape)
+    lengths[split] = width
+    height = lengths[join]
+    lengths[join] = height * ways
+    full = jnp.zeros(lengths, array.dtype)
+    for mask in range(ways):
+        part = lax.dynamic_slice_in_dim(array, (here ^ mask) * width, width, axis=split)
+        if mask:
+            part = lax.ppermute(part, axis, [(d, d ^ mask) for d in range(ways)])
+        full = lax.dynamic_update_slice_in_dim(full, part, (here ^ mask) * height, axis=join)
+    return full
 
 
 def passed_along(value, axis, steps):
@@ -144,7 +160,7 @@
     all_results = jnp.concatenate(results, axis=1).reshape(group_rows, HD)
     all_query_grads = jnp.concatenate(query_grads, axis=1).reshape(group_rows, HD)
     outputs, query_grad = (
-        lax.all_to_all(all_results, "head", split_axis=0, concat_axis=1, tiled=True),
+        swapped_with_each(all_results, "head", 0, 1),
         lax.all_to_all(all_query_grads, "head", split_axis=0, concat_axis=1, tiled=True),
     )
     wide_gk, wide_gv = (

time: 95.1 us -> 90 us (0.946)
  matrix products: 12.1 us -> 9.09 us
    ppermute x0 -> x3, waiting for transfers between devices: none -> 9.11 us  [swapped_with_each(): part = lax.ppermute(part, axis, [(d, d ^ mask) for d in range(ways)])]
    all_to_all x1, waiting for transfers between devices: 6.16 us -> 0.01 us  [per_device(): lax.all_to_all(own_v, 'head', split_axis=0, concat_axis=1, tiled=True)]
    all_to_all x1, waiting for transfers between devices: 2.12 us -> 7.28 us  [per_device(): lax.all_to_all(own_k, 'head', split_axis=0, concat_axis=1, tiled=True)]
    all_to_all x1, waiting for transfers between devices: 5.14 us -> 0.01 us  [per_device(): lax.all_to_all(all_query_grads, 'head', split_axis=0, concat_axis=1, tile...]
    all_to_all x1 -> x0, starting transfers between devices: 3.41 us -> none  [per_device(): lax.all_to_all(all_results, 'head', split_axis=0, concat_axis=1, tiled=True)]
    ppermute x4, waiting for transfers between devices: 3.34 us -> 0.01 us  [passed_along(): lax.ppermute(value, axis, [(source, source + steps) for source in range(f...]
    ppermute x0 -> x3, starting transfers between devices: none -> 2.5 us  [swapped_with_each(): part = lax.ppermute(part, axis, [(d, d ^ mask) for d in range(ways)])]
    dot_general x2, matrix products: 2.07 us -> 0.76 us  [attend(): lax.dot_general(grad_scores, key_block, forward, preferred_element_type=j...]
  transfers between devices with their start and end apart: 10 -> 12, of which waited for: 6 -> 5; matrix products, arithmetic and copies ran while one was open for 17% -> 12% of each run, Pallas kernels for 0% -> 0%
where the time goes in v1:
time: 90 us; the launch traced here: 88.8 us
  starting transfers between devices  32.5 us (36%)
  waiting for transfers between devices  25.2 us (28%)
  blocking collectives  11.9 us (13%)
  matrix products  9.09 us (10%)
  other arithmetic  4.72 us (5%)
  local copies, waits for them, and re-layouts  4.37 us (5%)
  between operations  1.06 us (1%)
    ppermute x4, starting transfers between devices, passed_along(): lax.ppermute(value, axis, [(source, source + steps) for source in range(f...  12.7 us
    ppermute x3, waiting for transfers between devices, swapped_with_each(): part = lax.ppermute(part, axis, [(d, d ^ mask) for d in range(ways)])  9.11 us
    all_to_all x1, waiting for transfers between devices, per_device(): lax.all_to_all(own_k, 'head', split_axis=0, concat_axis=1, tiled=True)  7.28 us
    all_gather x1, blocking collectives, per_device(): lax.all_gather(value_rows, 'head', axis=0, tiled=True)  6.13 us
    all_gather x1, blocking collectives, per_device(): lax.all_gather(key_rows, 'head', axis=0, tiled=True)  5.79 us
    all_to_all x1, waiting for transfers between devices, per_device(): lax.all_to_all(queries, 'head', split_axis=1, concat_axis=0, tiled=True)  5.51 us
    all_to_all x1, starting transfers between devices, per_device(): lax.all_to_all(out_grad, 'head', split_axis=1, concat_axis=0, tiled=True)  3.54 us
    all_to_all x1, starting transfers between devices, per_device(): lax.all_to_all(own_k, 'head', split_axis=0, concat_axis=1, tiled=True)  3.47 us
  transfers between devices with their start and end apart: 12, of which 5 were waited for; matrix products, arithmetic and copies ran while one was open for 12% of the time, Pallas kernels for 0%

profile of v1, /device:TPU:8, one launch (start us, length us, event | category | flops | bytes accessed | tf_op | source)
XLA Modules:
  0.0 88.8 jit_solution(10593506448366864819)
XLA Ops:
  0.6 0.0 copy-start.3
  0.6 6.1 %all_gather.7 = bf16[1024,128]{1,0:T(8,128)(2,1)S(1)} all-gather(bf16[256,128]{1,0:T(8,128)(2,1)} %param.19), channel_id=1, replica_groups=mesh['seq'=8,'head'=4] {'head'}, dimensions={0}, use_global_device_ids=true | all-gather | bytes 327680 | tf_op jit(solution)/shard_map/all_gather | solution.py:96
  6.8 3.5 %collective-permute-start.1 = (bf16[64,128]{1,0:T(8,128)(2,1)S(1)}, bf16[64,128]{1,0:T(8,128)(2,1)S(1)}, u32[]{:S(2)}, u32[]{:S(2)}) collective-permute-start(bf16[64,128]{1,0:T(8,128)(2,1)S(1)} %slice_bitcast_fusion.2), channel_id=1, source_target_pairs={{0,4},{4,8},{8,12},{12,16},{16,20},{20,24},{24,28},{1,5},{5,9},{9,... | collective-permute-start | bytes 49160 | tf_op jit(solution)/shard_map/ppermute | solution.py:32
  10.3 0.0 copy-done.3
  10.3 5.8 %all_gather.6 = bf16[1024,128]{1,0:T(8,128)(2,1)S(1)} all-gather(bf16[256,128]{1,0:T(8,128)(2,1)S(1)} %copy-done.3), channel_id=1, replica_groups=mesh['seq'=8,'head'=4] {'head'}, dimensions={0}, use_global_device_ids=true | all-gather | bytes 327680 | tf_op jit(solution)/shard_map/all_gather | solution.py:95
  16.1 3.4 %collective-permute-start = (bf16[64,128]{1,0:T(8,128)(2,1)S(1)}, bf16[64,128]{1,0:T(8,128)(2,1)S(1)}, u32[]{:S(2)}, u32[]{:S(2)}) collective-permute-start(bf16[64,128]{1,0:T(8,128)(2,1)S(1)} %slice_bitcast_fusion.3), channel_id=1, source_target_pairs={{0,4},{4,8},{8,12},{12,16},{16,20},{20,24},{24,28},{1,5},{5,9},{9,... | collective-permute-start | bytes 49160 | tf_op jit(solution)/shard_map/ppermute | solution.py:32
  19.6 0.0 copy-done
  19.6 0.1 copy.11
  19.7 0.8 copy.12
  20.6 3.5 %all-to-all-start.1 = ((bf16[256,4,128]{2,0,1:T(8,128)(2,1)}), bf16[256,4,128]{2,0,1:T(8,128)(2,1)S(1)}, u32[]{:S(2)}, u32[]{:S(2)}) async-start(bf16[256,4,128]{2,0,1:T(8,128)(2,1)} %copy.12), calls=%async_computation.1 | async-start | bytes 524288 | tf_op jit(solution)/shard_map/all_to_all | solution.py:92
  24.1 0.0 copy-start.1
  24.2 0.0 copy-done.4
  24.2 0.1 dynamic_slice.20
  24.3 0.6 dynamic_slice.21
  24.9 0.1 iota_compare_fusion.1
  24.9 0.1 broadcast_compare_fusion
  25.1 0.7 add_add_fusion
  25.8 0.0 copy-done.1
  25.8 0.1 copy.9
  26.0 0.8 copy.10
  26.8 3.3 %all-to-all-done.1 = bf16[256,4,128]{2,0,1:T(8,128)(2,1)S(1)} async-done(((bf16[256,4,128]{2,0,1:T(8,128)(2,1)}), bf16[256,4,128]{2,0,1:T(8,128)(2,1)S(1)}, u32[]{:S(2)}, u32[]{:S(2)}) %all-to-all-start.1) | async-done | bytes 262176 | tf_op jit(solution)/shard_map/all_to_all | solution.py:92
  30.1 3.4 %all-to-all-start = ((bf16[256,4,128]{2,0,1:T(8,128)(2,1)}), bf16[256,4,128]{2,0,1:T(8,128)(2,1)S(1)}, u32[]{:S(2)}, u32[]{:S(2)}) async-start(bf16[256,4,128]{2,0,1:T(8,128)(2,1)} %copy.10), calls=%async_computation | async-start | bytes 524288 | tf_op jit(solution)/shard_map/all_to_all | solution.py:91
  33.5 0.0 collective-permute-done.1
  33.5 0.2 convolution_bitcast_fusion
  33.8 0.2 convolution_bitcast_fusion.1
  34.0 0.0 collective-permute-done
  34.0 5.5 %all-to-all-done = bf16[256,4,128]{2,0,1:T(8,128)(2,1)S(1)} async-done(((bf16[256,4,128]{2,0,1:T(8,128)(2,1)}), bf16[256,4,128]{2,0,1:T(8,128)(2,1)S(1)}, u32[]{:S(2)}, u32[]{:S(2)}) %all-to-all-start) | async-done | bytes 262176 | tf_op jit(solution)/shard_map/all_to_all | solution.py:91
  39.5 0.5 fusion.106
  40.0 0.7 convolution_convert_fusion.3
  40.7 0.3 convolution_convert_fusion.1
  41.0 0.3 fusion.22
  41.3 1.3 %fusion.43 = f32[4,192,128]{2,1,0:T(8,128)} fusion(bf16[4,256,128]{2,1,0:T(8,128)(2,1)S(1)} %bitcast.71, f32[4,128]{1,0:T(4,128)S(1)} %get-tuple-element.78, bf16[4,256,128]{2,1,0:T(8,128)(2,1)S(1)} %bitcast.90, bf16[4,256,128]{2,1,0:T(8,128)(2,1)S(1)} %bitcast.82, bf16[3,64,128]{2,1,0:T(8,128)(2,1)S(1)} %slice.163, bf16[1,64,128]{2,1,0:T(8,128)(2,1)S(1)} %bitcast.104, ...), kind=kOutput, calls=%fused_computation.65 | convolution fusion | flops 53084864 | bytes 1040384 | tf_op jit(solution)/shard_map/dot_general | solution.py:76
  42.6 0.7 fusion.103
  43.3 0.0 copy-start.5
  43.3 0.9 %convolution_convert_fusion.2 = bf16[4,128,128]{2,1,0:T(8,128)(2,1)S(1)} fusion(bf16[4,256,128]{2,1,0:T(8,128)(2,1)S(1)} %bitcast.67, bf16[3,64,128]{2,1,0:T(8,128)(2,1)S(1)} %slice.166, bf16[1,64,128]{2,1,0:T(8,128)(2,1)S(1)} %bitcast.98, f32[4,128]{1,0:T(4,128)S(1)} %get-tuple-element.76, bf16[4,256,128]{2,1,0:T(8,128)(2,1)S(1)} %bitcast.84, ...), kind=kOutput, calls=%fused_computation.30 | convolution fusion | flops 89523008 | bytes 1010688 | tf_op jit(solution)/shard_map/dot_general | solution.py:62
  44.3 0.0 copy-done.5
  44.3 0.4 convolution_convert_fusion
  44.7 0.7 pad_maximum_fusion.5
  45.4 3.4 %all-to-all-start.2 = ((bf16[4,256,128]{2,1,0:T(8,128)(2,1)}), bf16[4,256,128]{2,1,0:T(8,128)(2,1)S(1)}, u32[]{:S(2)}, u32[]{:S(2)}) async-start(bf16[4,256,128]{2,1,0:T(8,128)(2,1)} %pad_maximum_fusion.5), calls=%async_computation.2 | async-start | bytes 524288 | tf_op jit(solution)/shard_map/all_to_all | solution.py:164
  48.9 1.6 %convolution_add_fusion.1 = f32[4,320,128]{2,1,0:T(8,128)S(1)} fusion(f32[4,128,320]{1,2,0:T(8,128)S(1)} %convolution_bitcast_fusion, f32[4,192,128]{2,1,0:T(8,128)S(1)} %fusion.22, bf16[4,256,128]{2,1,0:T(8,128)(2,1)S(1)} %bitcast.93, f32[4,128,320]{1,2,0:T(8,128)} %copy-done.5, f32[4,128]{1,0:T(4,128)S(1)} %get-tuple-element.76), kind=kOutput, calls=%fused_computation.11 | convolution fusion | flops 43254592 | bytes 3805184 | tf_op jit(solution)/shard_map/dot_general | solution.py:73
  50.5 3.3 %collective-permute-start.5 = (f32[64,128]{1,0:T(8,128)S(1)}, f32[64,128]{1,0:T(8,128)S(1)}, u32[]{:S(2)}, u32[]{:S(2)}) collective-permute-start(f32[64,128]{1,0:T(8,128)S(1)} %slice_bitcast_fusion.1), channel_id=1, source_target_pairs={{4,0},{8,4},{12,8},{16,12},{20,16},{24,20},{28,24},{5,1},{9,5},{13... | collective-permute-start | bytes 98312 | tf_op jit(solution)/shard_map/ppermute | solution.py:32
  53.8 1.8 %convolution_add_fusion = f32[4,320,128]{2,1,0:T(8,128)S(1)} fusion(f32[4,192,128]{2,1,0:T(8,128)} %fusion.43, bf16[4,256,128]{2,1,0:T(8,128)(2,1)S(1)} %bitcast.72, f32[4,128]{1,0:T(4,128)S(1)} %get-tuple-element.76, bf16[4,256,128]{2,1,0:T(8,128)(2,1)S(1)} %bitcast.86, bf16[3,64,128]{2,1,0:T(8,128)(2,1)S(1)} %slice.163, ...), kind=kOutput, calls=%fused_computation.10 | convolution fusion | flops 88638272 | bytes 1731584 | tf_op jit(solution)/shard_map/dot_general | solution.py:76
  55.7 2.4 %collective-permute-start.6 = (f32[64,128]{1,0:T(8,128)S(1)}, f32[64,128]{1,0:T(8,128)S(1)}, u32[]{:S(2)}, u32[]{:S(2)}) collective-permute-start(f32[64,128]{1,0:T(8,128)S(1)} %slice_bitcast_fusion), channel_id=1, source_target_pairs={{4,0},{8,4},{12,8},{16,12},{20,16},{24,20},{28,24},{5,1},{9,5},{13... | collective-permute-start | bytes 98312 | tf_op jit(solution)/shard_map/ppermute | solution.py:32
  58.2 0.0 collective-permute-done.5
  58.2 0.8 pad_maximum_fusion
  59.0 0.0 all-to-all-done.2
  59.0 3.5 %all-to-all-start.3 = ((f32[4,256,128]{2,1,0:T(8,128)}), f32[4,256,128]{2,1,0:T(8,128)S(1)}, u32[]{:S(2)}, u32[]{:S(2)}) async-start(f32[4,256,128]{2,1,0:T(8,128)} %pad_maximum_fusion), calls=%async_computation.3 | async-start | bytes 1048576 | tf_op jit(solution)/shard_map/all_to_all | solution.py:167
  62.6 0.5 collective-permute-start.2
  63.2 0.0 collective-permute-done.6
  63.2 0.8 pad_maximum_fusion.1
  64.0 7.3 %all-to-all-done.3 = f32[4,256,128]{2,1,0:T(8,128)S(1)} async-done(((f32[4,256,128]{2,1,0:T(8,128)}), f32[4,256,128]{2,1,0:T(8,128)S(1)}, u32[]{:S(2)}, u32[]{:S(2)}) %all-to-all-start.3) | async-done | bytes 524320 | tf_op jit(solution)/shard_map/all_to_all | solution.py:167
  71.3 3.5 %all-to-all-start.4 = ((f32[4,256,128]{2,1,0:T(8,128)}), f32[4,256,128]{2,1,0:T(8,128)S(1)}, u32[]{:S(2)}, u32[]{:S(2)}) async-start(f32[4,256,128]{2,1,0:T(8,128)} %pad_maximum_fusion.1), calls=%async_computation.4 | async-start | bytes 1048576 | tf_op jit(solution)/shard_map/all_to_all | solution.py:168
  74.8 2.0 %collective-permute-start.3 = (bf16[256,128]{1,0:T(8,128)(2,1)S(1)}, bf16[256,128]{1,0:T(8,128)(2,1)S(1)}, u32[]{:S(2)}, u32[]{:S(2)}) collective-permute-start(bf16[256,128]{1,0:T(8,128)(2,1)S(1)} %get-tuple-element.73), channel_id=1, source_target_pairs={{0,2},{1,3},{2,0},{3,1},{4,6},{5,7},{6,4},{7,5},{8,10},{9,11},{10,... | collective-permute-start | bytes 196616 | tf_op jit(solution)/shard_map/ppermute | solution.py:24
  76.8 0.0 collective-permute-start.4
  76.8 0.0 collective-permute-done.2
  76.8 8.7 %collective-permute-done.3 = bf16[256,128]{1,0:T(8,128)(2,1)S(1)} collective-permute-done((bf16[256,128]{1,0:T(8,128)(2,1)S(1)}, bf16[256,128]{1,0:T(8,128)(2,1)S(1)}, u32[]{:S(2)}, u32[]{:S(2)}) %collective-permute-start.3) | collective-permute-done | bytes 65568 | tf_op jit(solution)/shard_map/ppermute | solution.py:24
  85.5 0.4 collective-permute-done.4
  86.0 0.0 copy-start.2
  86.0 0.1 copy.13
  86.1 0.5 copy-done.2
  86.7 0.8 copy.14
  87.5 0.7 reduce_sum.58
  88.2 0.0 all-to-all-done.4
  88.2 0.7 reduce_sum.59
  (26 shorter events, 0.3 us)
Async XLA Ops:
  0.6 9.7 %copy-start.3 = (bf16[256,128]{1,0:T(8,128)(2,1)S(1)}, bf16[256,128]{1,0:T(8,128)(2,1)}, u32[]{:S(2)}) copy-start(bf16[256,128]{1,0:T(8,128)(2,1)} %param.18) | copy-start | bytes 196612
  6.8 12.8 %copy-start = (bf16[256,512]{1,0:T(8,128)(2,1)S(1)}, bf16[256,512]{1,0:T(8,128)(2,1)}, u32[]{:S(2)}) copy-start(bf16[256,512]{1,0:T(8,128)(2,1)} %param.20) | copy-start | bytes 786436
  6.8 26.7 %collective-permute-start.1 = (bf16[64,128]{1,0:T(8,128)(2,1)S(1)}, bf16[64,128]{1,0:T(8,128)(2,1)S(1)}, u32[]{:S(2)}, u32[]{:S(2)}) collective-permute-start(bf16[64,128]{1,0:T(8,128)(2,1)S(1)} %slice_bitcast_fusion.2), channel_id=1, source_target_pairs={{0,4},{4,8},{8,12},{12,16},{16,20},{20,24},{24,28},{1,5},{5,9},{9,... | collective-permute-start | bytes 49160 | tf_op jit(solution)/shard_map/ppermute | solution.py:32
  16.1 17.9 %collective-permute-start = (bf16[64,128]{1,0:T(8,128)(2,1)S(1)}, bf16[64,128]{1,0:T(8,128)(2,1)S(1)}, u32[]{:S(2)}, u32[]{:S(2)}) collective-permute-start(bf16[64,128]{1,0:T(8,128)(2,1)S(1)} %slice_bitcast_fusion.3), channel_id=1, source_target_pairs={{0,4},{4,8},{8,12},{12,16},{16,20},{20,24},{24,28},{1,5},{5,9},{9,... | collective-permute-start | bytes 49160 | tf_op jit(solution)/shard_map/ppermute | solution.py:32
  20.5 3.6 %copy-start.4 = (s32[32]{0:T(128)S(1)}, s32[32]{0:T(128)}, u32[]{:S(2)}) copy-start(s32[32]{0:T(128)} %param.21) | copy-start | bytes 388
  20.6 9.5 %all-to-all-start.1 = ((bf16[256,4,128]{2,0,1:T(8,128)(2,1)}), bf16[256,4,128]{2,0,1:T(8,128)(2,1)S(1)}, u32[]{:S(2)}, u32[]{:S(2)}) async-start(bf16[256,4,128]{2,0,1:T(8,128)(2,1)} %copy.12), calls=%async_computation.1 | async-start | bytes 524288 | tf_op jit(solution)/shard_map/all_to_all | solution.py:92
  24.1 1.7 %copy-start.1 = (bf16[256,512]{1,0:T(8,128)(2,1)S(1)}, bf16[256,512]{1,0:T(8,128)(2,1)}, u32[]{:S(2)}) copy-start(bf16[256,512]{1,0:T(8,128)(2,1)} %param.17) | copy-start | bytes 786436
  30.1 9.4 %all-to-all-start = ((bf16[256,4,128]{2,0,1:T(8,128)(2,1)}), bf16[256,4,128]{2,0,1:T(8,128)(2,1)S(1)}, u32[]{:S(2)}, u32[]{:S(2)}) async-start(bf16[256,4,128]{2,0,1:T(8,128)(2,1)} %copy.10), calls=%async_computation | async-start | bytes 524288 | tf_op jit(solution)/shard_map/all_to_all | solution.py:91
  43.3 1.0 %copy-start.5 = (f32[4,128,320]{1,2,0:T(8,128)}, f32[4,128,320]{1,2,0:T(8,128)S(1)}, u32[]{:S(2)}) copy-start(f32[4,128,320]{1,2,0:T(8,128)S(1)} %get-tuple-element.77) | copy-start | bytes 1966084
  45.4 13.6 %all-to-all-start.2 = ((bf16[4,256,128]{2,1,0:T(8,128)(2,1)}), bf16[4,256,128]{2,1,0:T(8,128)(2,1)S(1)}, u32[]{:S(2)}, u32[]{:S(2)}) async-start(bf16[4,256,128]{2,1,0:T(8,128)(2,1)} %pad_maximum_fusion.5), calls=%async_computation.2 | async-start | bytes 524288 | tf_op jit(solution)/shard_map/all_to_all | solution.py:164
  50.5 7.7 %collective-permute-start.5 = (f32[64,128]{1,0:T(8,128)S(1)}, f32[64,128]{1,0:T(8,128)S(1)}, u32[]{:S(2)}, u32[]{:S(2)}) collective-permute-start(f32[64,128]{1,0:T(8,128)S(1)} %slice_bitcast_fusion.1), channel_id=1, source_target_pairs={{4,0},{8,4},{12,8},{16,12},{20,16},{24,20},{28,24},{5,1},{9,5},{13... | collective-permute-start | bytes 98312 | tf_op jit(solution)/shard_map/ppermute | solution.py:32
  55.7 7.5 %collective-permute-start.6 = (f32[64,128]{1,0:T(8,128)S(1)}, f32[64,128]{1,0:T(8,128)S(1)}, u32[]{:S(2)}, u32[]{:S(2)}) collective-permute-start(f32[64,128]{1,0:T(8,128)S(1)} %slice_bitcast_fusion), channel_id=1, source_target_pairs={{4,0},{8,4},{12,8},{16,12},{20,16},{24,20},{28,24},{5,1},{9,5},{13... | collective-permute-start | bytes 98312 | tf_op jit(solution)/shard_map/ppermute | solution.py:32
  59.0 12.3 %all-to-all-start.3 = ((f32[4,256,128]{2,1,0:T(8,128)}), f32[4,256,128]{2,1,0:T(8,128)S(1)}, u32[]{:S(2)}, u32[]{:S(2)}) async-start(f32[4,256,128]{2,1,0:T(8,128)} %pad_maximum_fusion), calls=%async_computation.3 | async-start | bytes 1048576 | tf_op jit(solution)/shard_map/all_to_all | solution.py:167
  62.6 14.2 %collective-permute-start.2 = (bf16[256,128]{1,0:T(8,128)(2,1)S(1)}, bf16[256,128]{1,0:T(8,128)(2,1)S(1)}, u32[]{:S(2)}, u32[]{:S(2)}) collective-permute-start(bf16[256,128]{1,0:T(8,128)(2,1)S(1)} %get-tuple-element.74), channel_id=1, source_target_pairs={{0,1},{1,0},{2,3},{3,2},{4,5},{5,4},{6,7},{7,6},{8,9},{9,8},{10,11... | collective-permute-start | bytes 196616 | tf_op jit(solution)/shard_map/ppermute | solution.py:24
  71.3 16.9 %all-to-all-start.4 = ((f32[4,256,128]{2,1,0:T(8,128)}), f32[4,256,128]{2,1,0:T(8,128)S(1)}, u32[]{:S(2)}, u32[]{:S(2)}) async-start(f32[4,256,128]{2,1,0:T(8,128)} %pad_maximum_fusion.1), calls=%async_computation.4 | async-start | bytes 1048576 | tf_op jit(solution)/shard_map/all_to_all | solution.py:168
  74.8 10.7 %collective-permute-start.3 = (bf16[256,128]{1,0:T(8,128)(2,1)S(1)}, bf16[256,128]{1,0:T(8,128)(2,1)S(1)}, u32[]{:S(2)}, u32[]{:S(2)}) collective-permute-start(bf16[256,128]{1,0:T(8,128)(2,1)S(1)} %get-tuple-element.73), channel_id=1, source_target_pairs={{0,2},{1,3},{2,0},{3,1},{4,6},{5,7},{6,4},{7,5},{8,10},{9,11},{10,... | collective-permute-start | bytes 196616 | tf_op jit(solution)/shard_map/ppermute | solution.py:24
  76.8 9.2 %collective-permute-start.4 = (bf16[256,128]{1,0:T(8,128)(2,1)S(1)}, bf16[256,128]{1,0:T(8,128)(2,1)S(1)}, u32[]{:S(2)}, u32[]{:S(2)}) collective-permute-start(bf16[256,128]{1,0:T(8,128)(2,1)S(1)} %get-tuple-element.72), channel_id=1, source_target_pairs={{0,3},{1,2},{2,1},{3,0},{4,7},{5,6},{6,5},{7,4},{8,11},{9,10},{10,... | collective-permute-start | bytes 196616 | tf_op jit(solution)/shard_map/ppermute | solution.py:24
  86.0 0.7 copy-start.2
